TPU v7x, 32 devices: a whole 2x2x4 slice. The times are simulated.
32 devices in a mesh: state: 4 (over z), basis: 8 (over y, x, core).
Axes of the slice: x: 2, y: 2, z: 4, core: 2. Of those that a mesh axis runs over, the one named last changes fastest.
Arguments:
- states: float32 [8, 64, 64000], P('state', 'basis'), may hold values from -40 to 40
- membrane_step: float32 [40, 40], replicated, may hold values from -1 to 1
- cavity_forward: float32 [64, 64], replicated, may hold values from -0.75 to 0.75
- coupling: float32 [64, 40], replicated, may hold values from 0.25 to 1
- membrane_forward: float32 [40, 40], replicated, may hold values from -1 to 1
- cavity_back: float32 [64, 64], replicated, may hold values from -9 to 9
- membrane_back: float32 [40, 40], replicated, may hold values from -1 to 1
Outputs:
- orthonormal: float32 [8, 64, 64000], P('state', 'basis')
All inputs are finite; a program needn't handle non-finite values.
Results may differ from a plain program's by a relative error of at most 0.000075.
Values sent between devices are 32-bit elements; how exact they have to be, the bound alone decides.
A program may use at most 192 MiB of HBM per device.

v0:
```python
import jax
import jax.numpy as jnp
from jax import lax
from jax.sharding import PartitionSpec as P


def body(
    states, membrane_step, cavity_forward, coupling, membrane_forward, cavity_back, membrane_back
):
    highest = lax.Precision.HIGHEST
    panel_size, level_count, joint = states.shape
    levels_all = cavity_forward.shape[0]
    membrane_levels = membrane_step.shape[0]
    basis_total = float(levels_all * joint)
    head = jnp.einsum(
        "ab,scbr->scar",
        membrane_step,
        states.reshape(panel_size, level_count, membrane_levels, joint // membrane_levels),
        precision=highest,
    )
    head = head.reshape(panel_size, level_count, joint)
    panel_block = lax.all_to_all(head, "basis", split_axis=2, concat_axis=1, tiled=True)
    items, cavity_all, columns = panel_block.shape
    grid = jnp.einsum("qc,kcr->kqr", cavity_forward, panel_block, precision=highest)
    grid = jnp.einsum(
        "kqtm,nm->kqtn",
        grid.reshape(items, cavity_all, columns // membrane_levels, membrane_levels),
        membrane_forward,
        precision=highest,
    )
    weighted = grid * coupling[None, :, None, :]
    backward = jnp.einsum("kqtn,mn->kqtm", weighted, membrane_back, precision=highest)
    backward = backward.reshape(items, cavity_all, columns)
    stepped = jnp.einsum("cq,kqr->kcr", cavity_back, backward, precision=highest)
    spread = lax.all_to_all(stepped, "state", split_axis=2, concat_axis=0, tiled=True)
    state_total, spread_levels, spread_cols = spread.shape
    flattened = spread.reshape(state_total, -1)
    partial_gram = jnp.dot(flattened, flattened.T, precision=highest)
    gram = lax.psum(partial_gram, ("state", "basis")) / basis_total
    lower_factor = jnp.linalg.cholesky(gram)
    identity = jnp.eye(state_total, dtype=gram.dtype)
    inverse = lax.linalg.triangular_solve(lower_factor, identity, left_side=True, lower=True)
    local_result = jnp.dot(inverse, flattened, precision=highest)
    local_result = local_result.reshape(state_total, spread_levels, spread_cols)
    return lax.all_to_all(
        lax.all_to_all(local_result, "state", split_axis=0, concat_axis=2, tiled=True),
        "basis",
        split_axis=1,
        concat_axis=2,
        tiled=True,
    )


def solution(mesh):
    in_specs = (P("state", "basis", None), P(), P(), P(), P(), P(), P())
    out_specs = P("state", "basis", None)
    return jax.shard_map(body, mesh=mesh, in_specs=in_specs, out_specs=out_specs, check_vma=False)
```

profile of v0, /device:TPU:0, one launch (start us, length us, event | category | flops | bytes accessed | tf_op | source)
XLA Modules:
  0.0 946.3 jit_solution(17978958401633566701)
XLA Ops:
  0.0 0.0 copy-start
  0.0 4.5 reshape.28
  4.5 0.0 copy-done.3
  4.5 8.0 convolution_bitcast_fusion.2
  12.4 49.2 %copy.60 = f32[2,8,40,1600]{1,0,3,2:T(2,128)} copy(f32[2,8,40,1600]{3,2,1,0:T(8,128)} %convolution_bitcast_fusion.2) | data formatting | bytes 8192000 | tf_op jit(solution)/shard_map/reshape | solution.py:21
  61.6 137.2 %reshape.39 = f32[8,1,128000]{2,1,0:T(1,128)} reshape(f32[64000,2,8]{2,1,0:T(2,128)} %bitcast.76) | data formatting | bytes 8192000
  198.8 5.3 all-to-all-start
  204.1 0.1 copy.41
  204.2 48.1 %all-to-all-done = f32[8,1,128000]{2,1,0:T(1,128)} async-done(((f32[8,1,128000]{2,1,0:T(1,128)}), f32[8,1,128000]{2,1,0:T(1,128)}, u32[]{:S(2)}, u32[]{:S(2)}) %all-to-all-start) | async-done | bytes 4096032 | tf_op jit(solution)/shard_map/all_to_all | solution.py:22
  252.2 0.5 broadcast.49
  252.8 13.6 %reduce.6 = f32[8,128000]{1,0:T(8,128)} reduce(f32[8,1,128000]{2,1,0:T(1,128)} %all-to-all-done, f32[]{:T(128)} %broadcast.49), dimensions={1}, to_apply=%all_to_all.50.reduce_sub_computation | reduce | bytes 8192004 | tf_op jit(solution)/shard_map/all_to_all | solution.py:22
  266.4 142.2 %reshape.40 = f32[64000,2,8]{2,1,0:T(2,128)} reshape(f32[8,128000]{1,0:T(8,128)} %reduce.6) | data formatting | bytes 8192000
  408.6 71.1 %copy.38 = f32[2,8,8,8000]{3,1,2,0:T(8,128)} copy(f32[2,8,8,8000]{1,0,3,2:T(2,128)} %bitcast.77) | data formatting | bytes 8192000 | tf_op jit(solution)/shard_map/all_to_all | solution.py:22
  479.7 0.0 copy-done
  479.7 8.0 convolution_bitcast_fusion.1
  487.7 6.8 copy.39
  494.5 8.8 copy.40
  503.3 6.5 fusion.9
  509.8 7.1 fusion
  517.0 8.2 copy.42
  525.2 13.7 %convolution_bitcast_fusion = f32[2,64,8000]{2,1,0:T(8,128)} fusion(f32[2,64,8000]{1,2,0:T(8,128)} %bitcast.78, f32[64,64]{1,0:T(8,128)S(1)} %copy-done.2), kind=kOutput, calls=%fused_computation | convolution fusion | flops 786432000 | bytes 8208384 | tf_op jit(solution)/shard_map/cq,kqr->kcr/dot_general | solution.py:34
  538.9 10.7 %copy.44 = f32[2,64,8000]{1,0,2:T(2,128)} copy(f32[2,64,8000]{2,1,0:T(8,128)} %convolution_bitcast_fusion) | data formatting | bytes 8192000 | tf_op jit(solution)/shard_map/cq,kqr->kcr/transpose | solution.py:34
  549.6 11.3 %reshape.41 = f32[4,1,256000]{2,1,0:T(1,128)} reshape(f32[8000,2,64]{2,1,0:T(2,128)} %bitcast.81) | data formatting | bytes 8192000
  560.9 94.7 %all_to_all.69 = f32[4,1,256000]{2,1,0:T(1,128)} all-to-all(f32[4,1,256000]{2,1,0:T(1,128)} %reshape.41), channel_id=1, replica_groups=mesh['state'=4,'basis'=8] {'state'}, dimensions={0} | all-to-all | bytes 8192000 | tf_op jit(solution)/shard_map/all_to_all | solution.py:35
  655.6 14.4 %reduce.7 = f32[4,256000]{1,0:T(4,128)} reduce(f32[4,1,256000]{2,1,0:T(1,128)} %all_to_all.69, f32[]{:T(128)} %broadcast.49), dimensions={1}, to_apply=%all_to_all.54.reduce_sub_computation | reduce | bytes 8192004 | tf_op jit(solution)/shard_map/all_to_all | solution.py:35
  670.0 11.7 %reshape.42 = f32[8000,2,64]{2,1,0:T(2,128)} reshape(f32[4,256000]{1,0:T(4,128)} %reduce.7) | data formatting | bytes 8192000
  681.8 12.6 %copy.45 = f32[2,64,4,2000]{3,1,0,2:T(8,128)} copy(f32[2,64,4,2000]{1,0,3,2:T(2,128)} %bitcast.82) | data formatting | bytes 8192000 | tf_op jit(solution)/shard_map/all_to_all | solution.py:35
  694.3 7.5 reshape.32
  701.8 12.3 %fusion.15 = f32[8,8]{0,1:T(8,128)S(1)} fusion(f32[8,128000]{1,0:T(8,128)} %reshape.32), kind=kOutput, calls=%fused_computation.28 | convolution fusion | flops 98304000 | bytes 4096256 | tf_op jit(solution)/shard_map/dot_general | solution.py:38
  714.1 40.3 %psum.7 = f32[8,8]{0,1:T(8,128)S(1)} all-reduce(f32[8,8]{0,1:T(8,128)S(1)} %fusion.15), channel_id=1, replica_groups=mesh['state'=4,'basis'=8] {'state','basis'}, use_global_device_ids=true, to_apply=%region_0.0 | all-reduce | flops 64 | bytes 512 | tf_op jit(solution)/shard_map/psum | solution.py:39
  754.5 0.1 copy.47
  754.5 0.7 cholesky.17
  755.3 0.7 compare_reduce_fusion
  756.0 0.7 fusion.12
  756.7 0.6 custom-call.6
  757.3 0.2 convolution_bitcast_fusion.3
  757.5 7.5 dot_general.32
  765.0 7.8 fusion.2
  772.8 2.4 copy.50
  775.3 95.5 %all_to_all.70 = f32[8,64,2000]{2,1,0:T(8,128)S(1)} all-to-all(f32[8,64,2000]{2,1,0:T(8,128)S(1)} %copy.50), channel_id=1, replica_groups=mesh['state'=4,'basis'=8] {'state'}, dimensions={0} | all-to-all | bytes 8192000 | tf_op jit(solution)/shard_map/all_to_all | solution.py:46
  870.8 4.6 copy.65
  875.4 6.3 all_to_all.60
  881.7 5.4 copy.52
  887.1 51.7 %all_to_all.71 = f32[2,64,8000]{2,0,1:T(2,128)S(1)} all-to-all(f32[2,64,8000]{2,0,1:T(2,128)S(1)} %copy.52), channel_id=1, replica_groups=mesh['state'=4,'basis'=8] {'basis'}, dimensions={1} | all-to-all | bytes 8192000 | tf_op jit(solution)/shard_map/all_to_all | solution.py:45
  938.8 0.3 copy.66
  939.1 0.0 copy-start.1
  939.1 2.7 copy.54
  941.8 4.2 all_to_all.64
  (13 shorter events, 0.1 us)
Async XLA Ops:
  0.0 479.7 %copy-start = (f32[64,64]{1,0:T(8,128)S(1)}, f32[64,64]{1,0:T(8,128)}, u32[]{:S(2)}) copy-start(f32[64,64]{1,0:T(8,128)} %param.9) | copy-start | bytes 49156
  0.0 4.5 copy-start.3
  198.8 5.3 copy-start.6
  198.8 53.5 %all-to-all-start = ((f32[8,1,128000]{2,1,0:T(1,128)}), f32[8,1,128000]{2,1,0:T(1,128)}, u32[]{:S(2)}, u32[]{:S(2)}) async-start(f32[8,1,128000]{2,1,0:T(1,128)} %reshape.39), calls=%async_computation | async-start | bytes 8192000 | tf_op jit(solution)/shard_map/all_to_all | solution.py:22
  494.5 8.8 copy-start.4
  503.3 6.6 copy-start.5
  517.0 8.2 copy-start.2
  939.1 7.0 copy-start.1
where the time goes:
time: 958 us; the launch traced here: 946 us
  local copies, waits for them, and re-layouts  516 us (54%)
  blocking collectives  282 us (29%)
  matrix products  63.6 us (7%)
  waiting for transfers between devices  48.1 us (5%)
  other arithmetic  30.9 us (3%)
    unnamed x19, local copies, waits for them, and re-layouts  303 us
    all_to_all x1, blocking collectives, body(): lax.all_to_all(local_result, 'state', split_axis=0, concat_axis=2, tiled=...  95.5 us
    all_to_all x1, blocking collectives, body(): lax.all_to_all(stepped, 'state', split_axis=2, concat_axis=0, tiled=True)  94.7 us
    all_to_all x2, local copies, waits for them, and re-layouts, body(): lax.all_to_all(head, 'basis', split_axis=2, concat_axis=1, tiled=True)  71.6 us
    all_to_all x1, blocking collectives, body(): lax.all_to_all(lax.all_to_all(local_result, 'state', split_axis=0, concat...  51.7 us
    reshape x1, local copies, waits for them, and re-layouts, body(): head = head.reshape(panel_size, level_count, joint)  49.2 us
    all_to_all x1, waiting for transfers between devices, body(): lax.all_to_all(head, 'basis', split_axis=2, concat_axis=1, tiled=True)  48.1 us
    psum x1, blocking collectives, body(): gram = lax.psum(partial_gram, ('state', 'basis')) / basis_total  40.3 us
  transfers between devices with their start and end apart: 1, of which 1 were waited for; matrix products, arithmetic and copies ran while one was open for 0% of the time, Pallas kernels for 0%

commit v1 on v0

--- a/solution.py
+++ b/solution.py
@@ -19,7 +19,18 @@
         precision=highest,
     )
     head = head.reshape(panel_size, level_count, joint)
-    panel_block = lax.all_to_all(head, "basis", split_axis=2, concat_axis=1, tiled=True)
+
+    def connect_case(sheet):
+        base_arr = jax.lax.all_to_all(
+            jnp.stack(jnp.split(sheet, jax.lax.axis_size("basis"), axis=2), 0),
+            axis_name="basis",
+            split_axis=0,
+            concat_axis=0,
+        )
+        ready = jnp.concatenate(base_arr, 1)
+        return ready
+
+    panel_block = connect_case(head)
     items, cavity_all, columns = panel_block.shape
     grid = jnp.einsum("qc,kcr->kqr", cavity_forward, panel_block, precision=highest)
     grid = jnp.einsum(

time: 958 us -> 556 us (0.58)
  local copies, waits for them, and re-layouts: 516 us -> 132 us
  other arithmetic: 30.9 us -> 17.2 us
    unnamed x19 -> x26, local copies, waits for them, and re-layouts: 303 us -> 33.6 us
    all_to_all x2 -> x0, local copies, waits for them, and re-layouts: 71.6 us -> none  [body(): lax.all_to_all(head, 'basis', split_axis=2, concat_axis=1, tiled=True)]
    reshape x1, local copies, waits for them, and re-layouts: 49.2 us -> 4.25 us  [body(): head = head.reshape(panel_size, level_count, joint)]
    all_to_all x1 -> x0, other arithmetic: 13.6 us -> none  [body(): lax.all_to_all(head, 'basis', split_axis=2, concat_axis=1, tiled=True)]
where the time goes in v1:
time: 556 us; the launch traced here: 550 us
  blocking collectives  282 us (51%)
  local copies, waits for them, and re-layouts  132 us (24%)
  matrix products  63.5 us (11%)
  waiting for transfers between devices  48.3 us (9%)
  other arithmetic  17.2 us (3%)
  starting transfers between devices  5.85 us (1%)
    all_to_all x1, blocking collectives, body(): lax.all_to_all(local_result, 'state', split_axis=0, concat_axis=2, tiled=...  95.5 us
    all_to_all x1, blocking collectives, body(): lax.all_to_all(stepped, 'state', split_axis=2, concat_axis=0, tiled=True)  94.9 us
    all_to_all x1, blocking collectives, body(): lax.all_to_all(lax.all_to_all(local_result, 'state', split_axis=0, concat...  51.7 us
    all_to_all x1, waiting for transfers between devices, connect_case(): jax.lax.all_to_all(jnp.stack(jnp.split(sheet, jax.lax.axis_size('basis'),...  48.3 us
    psum x1, blocking collectives, body(): gram = lax.psum(partial_gram, ('state', 'basis')) / basis_total  40.3 us
    unnamed x26, local copies, waits for them, and re-layouts  33.6 us
    all_to_all x3, local copies, waits for them, and re-layouts, body(): lax.all_to_all(local_result, 'state', split_axis=0, concat_axis=2, tiled=...  16.3 us
    all_to_all x1, other arithmetic, body(): lax.all_to_all(stepped, 'state', split_axis=2, concat_axis=0, tiled=True)  14.4 us
  transfers between devices with their start and end apart: 1, of which 1 were waited for; matrix products, arithmetic and copies ran while one was open for 0% of the time, Pallas kernels for 0%

profile of v1, /device:TPU:0, one launch (start us, length us, event | category | flops | bytes accessed | tf_op | source)
XLA Modules:
  0.0 549.6 jit_solution(4596116572299702639)
XLA Ops:
  0.0 4.5 reshape.34
  4.5 7.9 %convolution_bitcast_fusion.2 = f32[2,8,40,1600]{3,2,1,0:T(8,128)} fusion(f32[2,8,40,1600]{3,2,1,0:T(8,128)} %reshape.34, f32[40,40]{1,0:T(8,128)S(1)} %copy-done.4), kind=kOutput, calls=%fused_computation.10 | convolution fusion | flops 491520000 | bytes 8198400 | tf_op jit(solution)/shard_map/ab,scbr->scar/dot_general | solution.py:15
  12.4 4.3 reshape.35
  16.7 2.0 fusion.14
  18.7 2.0 fusion.13
  20.7 1.9 fusion.12
  22.6 2.0 fusion.11
  24.6 0.8 fusion.10
  25.5 1.0 fusion.9
  26.5 0.8 fusion.8
  27.3 1.0 fusion.7
  28.3 5.8 %all-to-all-start = ((f32[8,2,8,8000]{3,2,1,0:T(8,128)}), f32[8,2,8,8000]{3,2,1,0:T(8,128)}, u32[]{:S(2)}, u32[]{:S(2)}) async-start(f32[8,2,8,8000]{3,2,1,0:T(8,128)} %fusion.7), calls=%async_computation | async-start | bytes 8257536 | tf_op jit(solution)/shard_map/all_to_all | solution.py:24
  34.1 0.1 copy.40
  34.2 48.3 %all-to-all-done = f32[8,2,8,8000]{3,2,1,0:T(8,128)} async-done(((f32[8,2,8,8000]{3,2,1,0:T(8,128)}), f32[8,2,8,8000]{3,2,1,0:T(8,128)}, u32[]{:S(2)}, u32[]{:S(2)}) %all-to-all-start) | async-done | bytes 4096032 | tf_op jit(solution)/shard_map/all_to_all | solution.py:24
  82.6 8.0 %convolution_bitcast_fusion.1 = f32[2,64,8000]{2,1,0:T(8,128)} fusion(f32[64,64]{1,0:T(8,128)S(1)} %copy-done, f32[8,2,8,8000]{3,2,1,0:T(8,128)} %all-to-all-done), kind=kOutput, calls=%fused_computation.1 | convolution fusion | flops 786432000 | bytes 8208384 | tf_op jit(solution)/shard_map/qc,kcr->kqr/dot_general | solution.py:35
  90.6 6.8 %copy.38 = f32[2,64,8000]{1,2,0:T(8,128)} copy(f32[2,64,8000]{2,1,0:T(8,128)} %convolution_bitcast_fusion.1) | data formatting | bytes 8192000 | tf_op jit(solution)/shard_map/qc,kcr->kqr/transpose | solution.py:35
  97.4 8.8 %copy.39 = f32[2,64,200,40]{2,3,1,0:T(8,128)} copy(f32[2,64,200,40]{1,3,2,0:T(8,128)} %bitcast.110) | data formatting | bytes 8192000 | tf_op jit(solution)/shard_map/reshape | solution.py:38
  106.2 6.5 %fusion.18 = f32[2,64,200,40]{2,3,1,0:T(8,128)S(1)} fusion(f32[2,64,200,40]{2,3,1,0:T(8,128)} %copy.39, f32[40,40]{1,0:T(8,128)S(1)} %copy-done.5), kind=kOutput, calls=%fused_computation.32 | convolution fusion | flops 491520000 | bytes 8198400 | tf_op jit(solution)/shard_map/kqtm,nm->kqtn/dot_general | solution.py:36
  112.7 7.0 %fusion = f32[2,64,200,40]{2,3,1,0:T(8,128)} fusion(f32[2,64,200,40]{2,3,1,0:T(8,128)S(1)} %fusion.18, f32[64,40]{1,0:T(8,128)S(1)} %copy.40, f32[40,40]{1,0:T(8,128)S(1)} %copy-done.6), kind=kOutput, calls=%fused_computation.2 | convolution fusion | flops 492544000 | bytes 8208640 | tf_op jit(solution)/shard_map/kqtn,mn->kqtm/dot_general | solution.py:43
  119.7 8.4 %copy.41 = f32[2,64,200,40]{1,3,2,0:T(8,128)} copy(f32[2,64,200,40]{2,3,1,0:T(8,128)} %fusion) | data formatting | bytes 8192000 | tf_op jit(solution)/shard_map/kqtn,mn->kqtm/dot_general | solution.py:43
  128.1 13.7 %convolution_bitcast_fusion = f32[2,64,8000]{2,1,0:T(8,128)} fusion(f32[2,64,8000]{1,2,0:T(8,128)} %bitcast.108, f32[64,64]{1,0:T(8,128)S(1)} %copy-done.3), kind=kOutput, calls=%fused_computation | convolution fusion | flops 786432000 | bytes 8208384 | tf_op jit(solution)/shard_map/cq,kqr->kcr/dot_general | solution.py:45
  141.8 10.7 %copy.43 = f32[2,64,8000]{1,0,2:T(2,128)} copy(f32[2,64,8000]{2,1,0:T(8,128)} %convolution_bitcast_fusion) | data formatting | bytes 8192000 | tf_op jit(solution)/shard_map/cq,kqr->kcr/transpose | solution.py:45
  152.5 11.1 %reshape.47 = f32[4,1,256000]{2,1,0:T(1,128)} reshape(f32[8000,2,64]{2,1,0:T(2,128)} %bitcast.111) | data formatting | bytes 8192000
  163.6 94.9 %all_to_all.56 = f32[4,1,256000]{2,1,0:T(1,128)} all-to-all(f32[4,1,256000]{2,1,0:T(1,128)} %reshape.47), channel_id=1, replica_groups=mesh['state'=4,'basis'=8] {'state'}, dimensions={0} | all-to-all | bytes 8192000 | tf_op jit(solution)/shard_map/all_to_all | solution.py:46
  258.5 0.5 broadcast.49
  259.0 14.4 %reduce.6 = f32[4,256000]{1,0:T(4,128)} reduce(f32[4,1,256000]{2,1,0:T(1,128)} %all_to_all.56, f32[]{:T(128)} %broadcast.49), dimensions={1}, to_apply=%all_to_all.41.reduce_sub_computation | reduce | bytes 8192004 | tf_op jit(solution)/shard_map/all_to_all | solution.py:46
  273.4 11.7 %reshape.48 = f32[8000,2,64]{2,1,0:T(2,128)} reshape(f32[4,256000]{1,0:T(4,128)} %reduce.6) | data formatting | bytes 8192000
  285.1 12.6 %copy.44 = f32[2,64,4,2000]{3,1,0,2:T(8,128)} copy(f32[2,64,4,2000]{1,0,3,2:T(2,128)} %bitcast.112) | data formatting | bytes 8192000 | tf_op jit(solution)/shard_map/all_to_all | solution.py:46
  297.6 7.5 %reshape.40 = f32[8,128000]{1,0:T(8,128)} reshape(f32[4,2,64,2000]{3,2,1,0:T(8,128)} %bitcast.113) | data formatting | bytes 8192000 | tf_op jit(solution)/shard_map/reshape | solution.py:48
  305.1 12.3 %fusion.24 = f32[8,8]{0,1:T(8,128)S(1)} fusion(f32[8,128000]{1,0:T(8,128)} %reshape.40), kind=kOutput, calls=%fused_computation.45 | convolution fusion | flops 98304000 | bytes 4096256 | tf_op jit(solution)/shard_map/dot_general | solution.py:49
  317.5 40.3 %psum.7 = f32[8,8]{0,1:T(8,128)S(1)} all-reduce(f32[8,8]{0,1:T(8,128)S(1)} %fusion.24), channel_id=1, replica_groups=mesh['state'=4,'basis'=8] {'state','basis'}, use_global_device_ids=true, to_apply=%region_0.0 | all-reduce | flops 64 | bytes 512 | tf_op jit(solution)/shard_map/psum | solution.py:50
  357.8 0.1 copy.46
  357.9 0.7 cholesky.17
  358.6 0.7 compare_reduce_fusion
  359.3 0.7 fusion.21
  360.0 0.6 custom-call.6
  360.7 0.2 convolution_bitcast_fusion.3
  360.8 7.5 %dot_general.32 = f32[64,2000,8]{1,0,2:T(8,128)} reshape(f32[128000,8]{0,1:T(8,128)} %bitcast.109) | data formatting | bytes 8192000 | tf_op jit(solution)/shard_map/dot_general | solution.py:54
  368.3 7.8 %fusion.2 = f32[8,64,2000]{2,0,1:T(8,128)S(1)} fusion(f32[8,8,1]{1,0,2:T(8,128)S(1)} %convolution_bitcast_fusion.3, f32[64,2000,8]{1,0,2:T(8,128)} %dot_general.32), kind=kOutput, calls=%fused_computation.5 | convolution fusion | flops 98304000 | bytes 8192256 | tf_op jit(solution)/shard_map/dot_general | solution.py:54
  376.2 2.4 copy.49
  378.6 95.5 %all_to_all.57 = f32[8,64,2000]{2,1,0:T(8,128)S(1)} all-to-all(f32[8,64,2000]{2,1,0:T(8,128)S(1)} %copy.49), channel_id=1, replica_groups=mesh['state'=4,'basis'=8] {'state'}, dimensions={0} | all-to-all | bytes 8192000 | tf_op jit(solution)/shard_map/all_to_all | solution.py:57
  474.1 4.6 copy.67
  478.7 6.3 %all_to_all.47 = f32[2,64,8000]{2,1,0:T(8,128)} reshape(f32[2,64,4,2000]{3,2,1,0:T(4,128)} %bitcast.115) | data formatting | bytes 8192000 | tf_op jit(solution)/shard_map/all_to_all | solution.py:57
  485.1 5.4 copy.51
  490.4 51.7 %all_to_all.58 = f32[2,64,8000]{2,0,1:T(2,128)S(1)} all-to-all(f32[2,64,8000]{2,0,1:T(2,128)S(1)} %copy.51), channel_id=1, replica_groups=mesh['state'=4,'basis'=8] {'basis'}, dimensions={1} | all-to-all | bytes 8192000 | tf_op jit(solution)/shard_map/all_to_all | solution.py:56
  542.1 0.3 copy.68
  542.4 2.7 copy.53
  545.1 4.2 all_to_all.51
  (19 shorter events, 0.1 us)
Async XLA Ops:
  0.0 82.6 %copy-start = (f32[64,64]{1,0:T(8,128)S(1)}, f32[64,64]{1,0:T(8,128)}, u32[]{:S(2)}) copy-start(f32[64,64]{1,0:T(8,128)} %param.9) | copy-start | bytes 49156
  0.0 4.5 copy-start.4
  16.7 8.0 %copy-start.2 = (f32[2,8,64000]{2,1,0:T(8,128)S(1)}, f32[2,8,64000]{2,1,0:T(8,128)}, u32[]{:S(2)}) copy-start(f32[2,8,64000]{2,1,0:T(8,128)} %reshape.35) | copy-start | bytes 12288004
  28.3 5.9 %copy-start.7 = (f32[64,40]{0,1:T(8,128)S(1)}, f32[64,40]{0,1:T(8,128)}, u32[]{:S(2)}) copy-start(f32[64,40]{0,1:T(8,128)} %param.10) | copy-start | bytes 30724
  28.3 54.3 %all-to-all-start = ((f32[8,2,8,8000]{3,2,1,0:T(8,128)}), f32[8,2,8,8000]{3,2,1,0:T(8,128)}, u32[]{:S(2)}, u32[]{:S(2)}) async-start(f32[8,2,8,8000]{3,2,1,0:T(8,128)} %fusion.7), calls=%async_computation | async-start | bytes 8257536 | tf_op jit(solution)/shard_map/all_to_all | solution.py:24
  97.4 8.8 %copy-start.5 = (f32[40,40]{1,0:T(8,128)S(1)}, f32[40,40]{1,0:T(8,128)}, u32[]{:S(2)}) copy-start(f32[40,40]{1,0:T(8,128)} %param.11) | copy-start | bytes 19204
  106.2 6.6 %copy-start.6 = (f32[40,40]{1,0:T(8,128)S(1)}, f32[40,40]{1,0:T(8,128)}, u32[]{:S(2)}) copy-start(f32[40,40]{1,0:T(8,128)} %param.13) | copy-start | bytes 19204
  119.7 8.4 %copy-start.3 = (f32[64,64]{1,0:T(8,128)S(1)}, f32[64,64]{1,0:T(8,128)}, u32[]{:S(2)}) copy-start(f32[64,64]{1,0:T(8,128)} %param.12) | copy-start | bytes 49156
  542.4 7.0 %copy-start.1 = (f32[64,64]{1,0:T(8,128)S(1)}, f32[64,64]{1,0:T(8,128)}, u32[]{:S(2)}) copy-start(f32[64,64]{1,0:T(8,128)} %param.9) | copy-start | bytes 49156
